TPU v7x, 256 devices: a whole 4x4x8 slice. The times are simulated.
256 devices in a mesh: dp: 4 (over x_hi, core), sx: 8 (over y, x_lo), syz: 8 (over z).
Axes of the slice: x: 4 (x_hi: 2, x_lo: 2; x = x_hi * 2 + x_lo), y: 4, z: 8, core: 2. Of those that a mesh axis runs over, the one named last changes fastest.
Arguments:
- input_act: bfloat16 [4, 32, 128, 64, 128], P('dp', 'sx', 'syz'), may hold values from -6 to 6
- pre_act: bfloat16 [4, 16, 64, 64, 128], P('dp', 'sx', 'syz'), may hold values from -6 to 6
- out_grad: bfloat16 [4, 8, 32, 32, 128], P('dp', 'sx', 'syz'), may hold values from -24 to 24
- weight_one: bfloat16 [3, 3, 3, 64, 128], replicated, may hold values from -0.15625 to 0.15625
- weight_two: bfloat16 [3, 3, 3, 128, 128], replicated, may hold values from -0.109375 to 0.109375
Outputs:
- grad_input: bfloat16 [4, 32, 128, 64, 128], P('dp', 'sx', 'syz')
- grad_one: float32 [3, 3, 3, 64, 128], replicated
- grad_two: float32 [3, 3, 3, 128, 128], replicated
All inputs are finite; a program needn't handle non-finite values.
Results may differ from a plain program's by a relative error of at most 0.0049.
Values may be sent and summed in bfloat16 or wider, within the bound.
No kernel may reach another device: no remote copies, remote signals or barrier semaphores. Data moves between devices by JAX's collectives and lax.ppermute only.
A program may use at most 64 MiB of HBM per device.

v0:
```python
import jax
import jax.numpy as jnp
from jax import lax
from jax.sharding import PartitionSpec as P


def from_behind(value, axis, steps):
    count = lax.axis_size(axis)
    initial, last = (max(0, -steps), min(count, count - steps))
    return lax.ppermute(value, axis, [(source, source + steps) for source in range(initial, last)])


def lower_rims(field):
    before_x = from_behind(field[-1:], "sx", 1)
    field = jnp.concatenate([before_x, field], axis=0)
    before_y = from_behind(field[:, -1:], "syz", 1)
    return jnp.concatenate([before_y, field], axis=1)


def upper_rims(field):
    after_x = from_behind(field[:1], "sx", -1)
    field = jnp.concatenate([field, after_x], axis=0)
    after_y = from_behind(field[:, :1], "syz", -1)
    return jnp.concatenate([field, after_y], axis=1)


def filter_grad(extended, cotangent, channels):
    count_x, count_y, count_z, width_out = cotangent.shape
    padded = jnp.pad(extended, ((0, 0), (0, 0), (1, 0), (0, 0)))
    pieces = []
    for kernel_x in range(3):
        for kernel_y in range(3):
            window = lax.slice(
                padded,
                (kernel_x, kernel_y, 0, 0),
                (kernel_x + 2 * count_x - 1, kernel_y + 2 * count_y - 1, count_z + 1, 2 * channels),
                (2, 2, 1, 1),
            )
            previous = jnp.einsum(
                "xyzc,xyzo->co",
                window[:, :, :-1, channels:],
                cotangent,
                preferred_element_type=jnp.float32,
            )
            current = jnp.einsum(
                "xyzc,xyzo->co", window[:, :, 1:], cotangent, preferred_element_type=jnp.float32
            ).reshape(2, channels, width_out)
            pieces.append(jnp.concatenate([previous[None], current], axis=0))
    return jnp.stack(pieces).reshape(3, 3, 3, channels, width_out)


def data_grad(extended, weights):
    count_x = extended.shape[0] - 1
    count_y = extended.shape[1] - 1
    width_in = weights.shape[3]
    width_out = weights.shape[4]
    padded = jnp.pad(extended, ((0, 0), (0, 0), (0, 1), (0, 0)))
    paired = jnp.concatenate([padded[:, :, :-1], padded[:, :, 1:]], axis=3)
    zeroes = jnp.zeros((width_out, width_in), weights.dtype)
    kernel_taps = (((1, 0),), ((2, 0), (0, 1)))
    planes = []
    for parity_x in range(2):
        columns = []
        for parity_y in range(2):
            summed = None
            for kernel_x, offset_x in kernel_taps[parity_x]:
                for kernel_y, offset_y in kernel_taps[parity_y]:
                    stencil = weights[kernel_x, kernel_y]
                    matrix = jnp.concatenate(
                        [
                            jnp.concatenate([stencil[1].T, stencil[2].T], axis=1),
                            jnp.concatenate([zeroes, stencil[0].T], axis=1),
                        ],
                        axis=0,
                    )
                    window = paired[offset_x : offset_x + count_x, offset_y : offset_y + count_y]
                    product = jnp.einsum(
                        "xyzk,kc->xyzc", window, matrix, preferred_element_type=jnp.float32
                    )
                    summed = product if summed is None else summed + product
            columns.append(summed)
        stacked = jnp.stack(columns, axis=2)
        planes.append(stacked.reshape(count_x, 2 * count_y, stacked.shape[3], stacked.shape[4]))
    assembled = jnp.stack(planes, axis=1)
    return assembled.reshape(2 * count_x, 2 * count_y, assembled.shape[3], assembled.shape[4])


def on_device(input_act, pre_act, out_grad, weight_one, weight_two):
    source = input_act[0]
    saved = pre_act[0]
    incoming = out_grad[0]
    channels_in = weight_one.shape[3]
    channels_mid = weight_one.shape[4]
    mid_x, mid_y, mid_z = (saved.shape[0], saved.shape[1], saved.shape[2])
    pre_float = saved.astype(jnp.float32)
    activation = jnp.where(pre_float > 0, pre_float, 0.3 * pre_float).astype(jnp.bfloat16)
    act_pairs = activation.reshape(mid_x, mid_y, mid_z // 2, 2 * channels_mid)
    grad_act = data_grad(upper_rims(incoming), weight_two).reshape(
        mid_x, mid_y, mid_z, channels_mid
    )
    grad_pre = (grad_act * jnp.where(pre_float > 0, 1.0, 0.3)).astype(jnp.bfloat16)
    grad_two = filter_grad(lower_rims(act_pairs), incoming, channels_mid)
    grad_one = filter_grad(lower_rims(source), grad_pre, channels_in)
    grad_input = data_grad(upper_rims(grad_pre), weight_one).astype(jnp.bfloat16)[None]
    devices_all = lax.axis_size("dp") * lax.axis_size("sx") * lax.axis_size("syz")
    cells_two = incoming.shape[0] * incoming.shape[1] * incoming.shape[2]
    grad_one = grad_one * float(devices_all * mid_x * mid_y * mid_z) ** (-0.5)
    grad_two = grad_two * float(devices_all * cells_two) ** (-0.5)
    grad_one, grad_two = lax.psum((grad_one, grad_two), ("dp", "sx", "syz"))
    return (grad_input, grad_one, grad_two)


def solution(mesh):
    in_specs = (
        P("dp", "sx", "syz", None, None),
        P("dp", "sx", "syz", None, None),
        P("dp", "sx", "syz", None, None),
        P(),
        P(),
    )
    out_specs = (P("dp", "sx", "syz", None, None), P(), P())
    return jax.shard_map(
        on_device, mesh=mesh, in_specs=in_specs, out_specs=out_specs, check_vma=False
    )
```

profile of v0, /device:TPU:8, one launch (start us, length us, event | category | flops | bytes accessed | tf_op | source)
XLA Modules:
  0.0 411.2 jit_solution(12811735037101333327)
XLA Ops:
  7.2 3.4 collective-permute-start
  10.6 2.0 copy.221
  13.5 2.5 collective-permute-start.4
  17.0 1.7 fusion.346
  20.4 1.3 collective-permute-start.1
  21.7 1.5 fusion.347
  23.2 1.4 copy.324
  24.6 1.4 copy.323
  26.0 1.4 copy.322
  27.4 1.5 copy.288
  28.9 1.5 copy.287
  30.4 1.5 copy.286
  31.9 1.5 copy.291
  33.3 1.5 copy.290
  34.8 1.5 copy.289
  36.3 1.5 copy.294
  37.7 1.5 copy.293
  39.2 1.5 copy.292
  41.4 1.5 copy.296
  78.3 4.2 %collective-permute-start.2 = (bf16[1,8,64,128]{3,2,1,0:T(8,128)(2,1)}, bf16[1,8,64,128]{3,2,1,0:T(8,128)(2,1)}, u32[]{:S(2)}, u32[]{:S(2)}) collective-permute-start(bf16[1,8,64,128]{3,2,1,0:T(8,128)(2,1)} %slice.659), channel_id=1, source_target_pairs={{8,0},{16,8},{24,16},{32,24},{40,32},{48,40},{56,48},{9,1},{17,9},... | collective-permute-start | bytes 393224 | tf_op jit(solution)/shard_map/ppermute | solution.py:10
  84.2 2.0 collective-permute-start.6
  87.3 4.6 %collective-permute-done.6 = bf16[1,8,32,256]{3,2,1,0:T(8,128)(2,1)S(1)} collective-permute-done((bf16[1,8,32,256]{3,2,1,0:T(8,128)(2,1)S(1)}, bf16[1,8,32,256]{3,2,1,0:T(8,128)(2,1)S(1)}, u32[]{:S(2)}, u32[]{:S(2)}) %collective-permute-start.6) | collective-permute-done | bytes 131104 | tf_op jit(solution)/shard_map/ppermute | solution.py:10
  91.9 4.5 %collective-permute-start.7 = (bf16[3,1,32,256]{3,2,1,0:T(8,128)(2,1)S(1)}, bf16[3,1,32,256]{3,2,1,0:T(8,128)(2,1)S(1)}, u32[]{:S(2)}, u32[]{:S(2)}) collective-permute-start(bf16[3,1,32,256]{3,2,1,0:T(8,128)(2,1)S(1)} %pad_maximum_fusion.8), channel_id=1, source_target_pairs={{0,1},{1,2},{2,3},{3,4},{4,5},{5,6},{6,7},{8,9},{9,10},{10,11},{11... | collective-permute-start | bytes 147464 | tf_op jit(solution)/shard_map/ppermute | solution.py:10
  104.3 2.1 fusion.187
  106.4 2.1 fusion.183
  108.5 1.4 broadcast_multiply_fusion
  110.7 4.3 %collective-permute-start.5 = (bf16[5,1,64,128]{2,3,1,0:T(8,128)(2,1)S(1)}, bf16[5,1,64,128]{2,3,1,0:T(8,128)(2,1)S(1)}, u32[]{:S(2)}, u32[]{:S(2)}) collective-permute-start(bf16[5,1,64,128]{2,3,1,0:T(8,128)(2,1)S(1)} %pad_maximum_fusion.6), channel_id=1, source_target_pairs={{0,1},{1,2},{2,3},{3,4},{4,5},{5,6},{6,7},{8,9},{9,10},{10,11},{11... | collective-permute-start | bytes 245768 | tf_op jit(solution)/shard_map/ppermute | solution.py:10
  115.0 2.1 fusion.179
  117.6 2.6 fusion.3
  131.3 1.4 fusion.12
  140.0 260.9 %all-reduce.25.cloned.1.call-done = (f32[3,3,3,64,128]{4,3,2,1,0:T(8,128)}, f32[3,3,3,128,128]{4,3,2,1,0:T(8,128)}) async-done(((f32[3,3,3,64,128]{4,3,2,1,0:T(8,128)}, f32[3,3,3,128,128]{4,3,2,1,0:T(8,128)}), (f32[3,3,3,64,128]{4,3,2,1,0:T(8,128)}, f32[3,3,3,128,128]{4,3,2,1,0:T(8,128)})) %all-reduce.25.cloned.1.call-update) | async-done | bytes 2654224 | tf_op jit(solution)/shard_map/psum | solution.py:109
  400.9 2.3 copy.388
  (331 shorter events, 69.6 us)
Async XLA Ops:
  7.2 393.7 %all-reduce.25.cloned.1.call-start = ((), (), s32[]{:S(2)}) async-start(), calls=%async_computation | async-start | bytes 5308416 | tf_op jit(solution)/shard_map/psum | solution.py:109
  7.2 12.5 %collective-permute-start = (bf16[1,4,32,128]{3,2,1,0:T(8,128)(2,1)}, bf16[1,4,32,128]{3,2,1,0:T(8,128)(2,1)S(1)}, u32[]{:S(2)}, u32[]{:S(2)}) collective-permute-start(bf16[1,4,32,128]{3,2,1,0:T(8,128)(2,1)} %bitcast.710), channel_id=1, source_target_pairs={{8,0},{16,8},{24,16},{32,24},{40,32},{48,40},{56,48},{9,1},{17,9},... | collective-permute-start | bytes 98312 | tf_op jit(solution)/shard_map/ppermute | solution.py:10
  13.5 96.4 %collective-permute-start.4 = (bf16[1,16,64,128]{2,3,1,0:T(8,128)(2,1)}, bf16[1,16,64,128]{2,3,1,0:T(8,128)(2,1)}, u32[]{:S(2)}, u32[]{:S(2)}) collective-permute-start(bf16[1,16,64,128]{2,3,1,0:T(8,128)(2,1)} %slice_bitcast_fusion), channel_id=1, source_target_pairs={{0,8},{8,16},{16,24},{24,32},{32,40},{40,48},{48,56},{1,9},{9,17},... | collective-permute-start | bytes 786440 | tf_op jit(solution)/shard_map/ppermute | solution.py:10
  19.5 23.4 %copy-start.7 = (bf16[1,1,1,128,128]{4,3,2,1,0:T(8,128)(2,1)S(1)}, bf16[1,1,1,128,128]{4,3,2,1,0:T(8,128)(2,1)}, u32[]{:S(2)}) copy-start(bf16[1,1,1,128,128]{4,3,2,1,0:T(8,128)(2,1)} %get-tuple-element.18) | copy-start | bytes 98308
  19.5 24.1 %copy-start.6 = (bf16[1,1,1,128,128]{4,3,2,1,0:T(8,128)(2,1)S(1)}, bf16[1,1,1,128,128]{4,3,2,1,0:T(8,128)(2,1)}, u32[]{:S(2)}) copy-start(bf16[1,1,1,128,128]{4,3,2,1,0:T(8,128)(2,1)} %get-tuple-element.31) | copy-start | bytes 98308
  19.6 24.8 %copy-start.5 = (bf16[1,1,1,128,128]{4,3,2,1,0:T(8,128)(2,1)S(1)}, bf16[1,1,1,128,128]{4,3,2,1,0:T(8,128)(2,1)}, u32[]{:S(2)}) copy-start(bf16[1,1,1,128,128]{4,3,2,1,0:T(8,128)(2,1)} %get-tuple-element.32) | copy-start | bytes 98308
  19.6 34.9 %copy-start.23 = (bf16[1,1,1,64,128]{4,3,2,1,0:T(8,128)(2,1)S(1)}, bf16[1,1,1,64,128]{4,3,2,1,0:T(8,128)(2,1)}, u32[]{:S(2)}) copy-start(bf16[1,1,1,64,128]{4,3,2,1,0:T(8,128)(2,1)} %get-tuple-element.55) | copy-start | bytes 49156
  19.6 35.6 %copy-start.22 = (bf16[1,1,1,64,128]{4,3,2,1,0:T(8,128)(2,1)S(1)}, bf16[1,1,1,64,128]{4,3,2,1,0:T(8,128)(2,1)}, u32[]{:S(2)}) copy-start(bf16[1,1,1,64,128]{4,3,2,1,0:T(8,128)(2,1)} %get-tuple-element.56) | copy-start | bytes 49156
  19.6 36.3 %copy-start.21 = (bf16[1,1,1,64,128]{4,3,2,1,0:T(8,128)(2,1)S(1)}, bf16[1,1,1,64,128]{4,3,2,1,0:T(8,128)(2,1)}, u32[]{:S(2)}) copy-start(bf16[1,1,1,64,128]{4,3,2,1,0:T(8,128)(2,1)} %get-tuple-element.57) | copy-start | bytes 49156
  19.6 37.0 %copy-start.20 = (bf16[1,1,1,64,128]{4,3,2,1,0:T(8,128)(2,1)S(1)}, bf16[1,1,1,64,128]{4,3,2,1,0:T(8,128)(2,1)}, u32[]{:S(2)}) copy-start(bf16[1,1,1,64,128]{4,3,2,1,0:T(8,128)(2,1)} %get-tuple-element.58) | copy-start | bytes 49156
  19.6 37.7 %copy-start.19 = (bf16[1,1,1,64,128]{4,3,2,1,0:T(8,128)(2,1)S(1)}, bf16[1,1,1,64,128]{4,3,2,1,0:T(8,128)(2,1)}, u32[]{:S(2)}) copy-start(bf16[1,1,1,64,128]{4,3,2,1,0:T(8,128)(2,1)} %get-tuple-element.59) | copy-start | bytes 49156
  19.6 38.4 %copy-start.18 = (bf16[1,1,1,64,128]{4,3,2,1,0:T(8,128)(2,1)S(1)}, bf16[1,1,1,64,128]{4,3,2,1,0:T(8,128)(2,1)}, u32[]{:S(2)}) copy-start(bf16[1,1,1,64,128]{4,3,2,1,0:T(8,128)(2,1)} %get-tuple-element.60) | copy-start | bytes 49156
  19.6 39.1 %copy-start.17 = (bf16[1,1,1,64,128]{4,3,2,1,0:T(8,128)(2,1)S(1)}, bf16[1,1,1,64,128]{4,3,2,1,0:T(8,128)(2,1)}, u32[]{:S(2)}) copy-start(bf16[1,1,1,64,128]{4,3,2,1,0:T(8,128)(2,1)} %get-tuple-element.61) | copy-start | bytes 49156
  19.6 39.2 %copy-start.16 = (bf16[1,1,1,64,128]{4,3,2,1,0:T(8,128)(2,1)S(1)}, bf16[1,1,1,64,128]{4,3,2,1,0:T(8,128)(2,1)}, u32[]{:S(2)}) copy-start(bf16[1,1,1,64,128]{4,3,2,1,0:T(8,128)(2,1)} %get-tuple-element.62) | copy-start | bytes 49156
  19.6 39.4 %copy-start.15 = (bf16[1,1,1,64,128]{4,3,2,1,0:T(8,128)(2,1)S(1)}, bf16[1,1,1,64,128]{4,3,2,1,0:T(8,128)(2,1)}, u32[]{:S(2)}) copy-start(bf16[1,1,1,64,128]{4,3,2,1,0:T(8,128)(2,1)} %get-tuple-element.63) | copy-start | bytes 49156
  19.7 39.5 %copy-start.14 = (bf16[1,1,1,64,128]{4,3,2,1,0:T(8,128)(2,1)S(1)}, bf16[1,1,1,64,128]{4,3,2,1,0:T(8,128)(2,1)}, u32[]{:S(2)}) copy-start(bf16[1,1,1,64,128]{4,3,2,1,0:T(8,128)(2,1)} %get-tuple-element.64) | copy-start | bytes 49156
  19.7 40.2 %copy-start.13 = (bf16[1,1,1,64,128]{4,3,2,1,0:T(8,128)(2,1)S(1)}, bf16[1,1,1,64,128]{4,3,2,1,0:T(8,128)(2,1)}, u32[]{:S(2)}) copy-start(bf16[1,1,1,64,128]{4,3,2,1,0:T(8,128)(2,1)} %get-tuple-element.65) | copy-start | bytes 49156
  19.7 40.9 %copy-start.12 = (bf16[1,1,1,64,128]{4,3,2,1,0:T(8,128)(2,1)S(1)}, bf16[1,1,1,64,128]{4,3,2,1,0:T(8,128)(2,1)}, u32[]{:S(2)}) copy-start(bf16[1,1,1,64,128]{4,3,2,1,0:T(8,128)(2,1)} %get-tuple-element.66) | copy-start | bytes 49156
  19.7 41.7 %copy-start.11 = (bf16[1,1,1,64,128]{4,3,2,1,0:T(8,128)(2,1)S(1)}, bf16[1,1,1,64,128]{4,3,2,1,0:T(8,128)(2,1)}, u32[]{:S(2)}) copy-start(bf16[1,1,1,64,128]{4,3,2,1,0:T(8,128)(2,1)} %get-tuple-element.67) | copy-start | bytes 49156
  19.7 42.4 %copy-start.10 = (bf16[1,1,1,64,128]{4,3,2,1,0:T(8,128)(2,1)S(1)}, bf16[1,1,1,64,128]{4,3,2,1,0:T(8,128)(2,1)}, u32[]{:S(2)}) copy-start(bf16[1,1,1,64,128]{4,3,2,1,0:T(8,128)(2,1)} %get-tuple-element.68) | copy-start | bytes 49156
  19.7 43.1 %copy-start.9 = (bf16[1,1,1,64,128]{4,3,2,1,0:T(8,128)(2,1)S(1)}, bf16[1,1,1,64,128]{4,3,2,1,0:T(8,128)(2,1)}, u32[]{:S(2)}) copy-start(bf16[1,1,1,64,128]{4,3,2,1,0:T(8,128)(2,1)} %get-tuple-element.69) | copy-start | bytes 49156
  19.7 43.8 %copy-start.8 = (bf16[1,1,1,64,128]{4,3,2,1,0:T(8,128)(2,1)S(1)}, bf16[1,1,1,64,128]{4,3,2,1,0:T(8,128)(2,1)}, u32[]{:S(2)}) copy-start(bf16[1,1,1,64,128]{4,3,2,1,0:T(8,128)(2,1)} %get-tuple-element.70) | copy-start | bytes 49156
  20.4 49.7 %collective-permute-start.1 = (bf16[2,1,32,128]{3,2,1,0:T(8,128)(2,1)}, bf16[2,1,32,128]{3,2,1,0:T(8,128)(2,1)S(1)}, u32[]{:S(2)}, u32[]{:S(2)}) collective-permute-start(bf16[2,1,32,128]{3,2,1,0:T(8,128)(2,1)} %pad_maximum_fusion.10), channel_id=1, source_target_pairs={{1,0},{2,1},{3,2},{4,3},{5,4},{6,5},{7,6},{9,8},{10,9},{11,10},{12... | collective-permute-start | bytes 49160 | tf_op jit(solution)/shard_map/ppermute | solution.py:10
  41.4 25.8 %copy-start.25 = (bf16[1,1,1,64,128]{4,3,2,1,0:T(8,128)(2,1)S(1)}, bf16[1,1,1,64,128]{4,3,2,1,0:T(8,128)(2,1)}, u32[]{:S(2)}) copy-start(bf16[1,1,1,64,128]{4,3,2,1,0:T(8,128)(2,1)} %get-tuple-element.76) | copy-start | bytes 49156
  41.4 26.5 %copy-start.24 = (bf16[1,1,1,64,128]{4,3,2,1,0:T(8,128)(2,1)S(1)}, bf16[1,1,1,64,128]{4,3,2,1,0:T(8,128)(2,1)}, u32[]{:S(2)}) copy-start(bf16[1,1,1,64,128]{4,3,2,1,0:T(8,128)(2,1)} %get-tuple-element.77) | copy-start | bytes 49156
  43.6 22.8 %copy-start.26 = (bf16[1,1,1,64,128]{4,3,2,1,0:T(8,128)(2,1)S(1)}, bf16[1,1,1,64,128]{4,3,2,1,0:T(8,128)(2,1)}, u32[]{:S(2)}) copy-start(bf16[1,1,1,64,128]{4,3,2,1,0:T(8,128)(2,1)} %get-tuple-element.75) | copy-start | bytes 49156
  48.0 23.3 %copy-start.54 = (bf16[1,1,1,128,128]{3,4,2,1,0:T(8,128)(2,1)S(1)}, bf16[1,1,1,128,128]{3,4,2,1,0:T(8,128)(2,1)}, u32[]{:S(2)}) copy-start(bf16[1,1,1,128,128]{3,4,2,1,0:T(8,128)(2,1)} %copy.291) | copy-start | bytes 98308
  78.3 18.2 %collective-permute-start.2 = (bf16[1,8,64,128]{3,2,1,0:T(8,128)(2,1)}, bf16[1,8,64,128]{3,2,1,0:T(8,128)(2,1)}, u32[]{:S(2)}, u32[]{:S(2)}) collective-permute-start(bf16[1,8,64,128]{3,2,1,0:T(8,128)(2,1)} %slice.659), channel_id=1, source_target_pairs={{8,0},{16,8},{24,16},{32,24},{40,32},{48,40},{56,48},{9,1},{17,9},... | collective-permute-start | bytes 393224 | tf_op jit(solution)/shard_map/ppermute | solution.py:10
  84.2 7.8 %collective-permute-start.6 = (bf16[1,8,32,256]{3,2,1,0:T(8,128)(2,1)S(1)}, bf16[1,8,32,256]{3,2,1,0:T(8,128)(2,1)S(1)}, u32[]{:S(2)}, u32[]{:S(2)}) collective-permute-start(bf16[1,8,32,256]{3,2,1,0:T(8,128)(2,1)S(1)} %slice.626), channel_id=1, source_target_pairs={{0,8},{8,16},{16,24},{24,32},{32,40},{40,48},{48,56},{1,9},{9,17},... | collective-permute-start | bytes 393224 | tf_op jit(solution)/shard_map/ppermute | solution.py:10
  91.9 6.6 %collective-permute-start.7 = (bf16[3,1,32,256]{3,2,1,0:T(8,128)(2,1)S(1)}, bf16[3,1,32,256]{3,2,1,0:T(8,128)(2,1)S(1)}, u32[]{:S(2)}, u32[]{:S(2)}) collective-permute-start(bf16[3,1,32,256]{3,2,1,0:T(8,128)(2,1)S(1)} %pad_maximum_fusion.8), channel_id=1, source_target_pairs={{0,1},{1,2},{2,3},{3,4},{4,5},{5,6},{6,7},{8,9},{9,10},{10,11},{11... | collective-permute-start | bytes 147464 | tf_op jit(solution)/shard_map/ppermute | solution.py:10
  97.2 6.0 %collective-permute-start.3 = (bf16[3,1,64,128]{3,2,1,0:T(8,128)(2,1)S(1)}, bf16[3,1,64,128]{3,2,1,0:T(8,128)(2,1)S(1)}, u32[]{:S(2)}, u32[]{:S(2)}) collective-permute-start(bf16[3,1,64,128]{3,2,1,0:T(8,128)(2,1)S(1)} %pad_maximum_fusion.9), channel_id=1, source_target_pairs={{1,0},{2,1},{3,2},{4,3},{5,4},{6,5},{7,6},{9,8},{10,9},{11,10},{12... | collective-permute-start | bytes 147464 | tf_op jit(solution)/shard_map/ppermute | solution.py:10
  110.7 6.9 %collective-permute-start.5 = (bf16[5,1,64,128]{2,3,1,0:T(8,128)(2,1)S(1)}, bf16[5,1,64,128]{2,3,1,0:T(8,128)(2,1)S(1)}, u32[]{:S(2)}, u32[]{:S(2)}) collective-permute-start(bf16[5,1,64,128]{2,3,1,0:T(8,128)(2,1)S(1)} %pad_maximum_fusion.6), channel_id=1, source_target_pairs={{0,1},{1,2},{2,3},{3,4},{4,5},{5,6},{6,7},{8,9},{9,10},{10,11},{11... | collective-permute-start | bytes 245768 | tf_op jit(solution)/shard_map/ppermute | solution.py:10
  (58 other events, 322.2 us)
Sparse Core Ops, SparseCore 0:
  129.4 271.4 all-reduce.24
where the time goes:
time: 413 us; the launch traced here: 411 us
  waiting for transfers between devices  267 us (65%)
  local copies, waits for them, and re-layouts  67.6 us (16%)
  matrix products  24.9 us (6%)
  starting transfers between devices  23.6 us (6%)
  between operations  15.7 us (4%)
  other arithmetic  13 us (3%)
    psum x1, waiting for transfers between devices, on_device(): grad_one, grad_two = lax.psum((grad_one, grad_two), ('dp', 'sx', 'syz'))  261 us
    unnamed x223, local copies, waits for them, and re-layouts  54.1 us
    ppermute x8, starting transfers between devices, from_behind(): lax.ppermute(value, axis, [(source, source + steps) for source in range(i...  23.5 us
    dot_general x18, matrix products, data_grad(): jnp.einsum('xyzk,kc->xyzc', window, matrix, preferred_element_type=jnp.fl...  16.9 us
  transfers between devices with their start and end apart: 9, of which 4 were waited for; matrix products, arithmetic and copies ran while one was open for 21% of the time, Pallas kernels for 0%

commit v1 on v0

--- a/solution.py
+++ b/solution.py
@@ -106,7 +106,7 @@
     cells_two = incoming.shape[0] * incoming.shape[1] * incoming.shape[2]
     grad_one = grad_one * float(devices_all * mid_x * mid_y * mid_z) ** (-0.5)
     grad_two = grad_two * float(devices_all * cells_two) ** (-0.5)
-    grad_one, grad_two = lax.psum((grad_one, grad_two), ("dp", "sx", "syz"))
+    grad_one, grad_two = lax.psum(lax.psum((grad_one, grad_two), ("sx", "syz")), "dp")
     return (grad_input, grad_one, grad_two)
 
 

time: 413 us -> 779 us (1.89)
  waiting for transfers between devices: 267 us -> 658 us
  local copies, waits for them, and re-layouts: 67.6 us -> 38.1 us
  starting transfers between devices: 23.6 us -> 35.1 us
  matrix products: 24.9 us -> 15.1 us
    psum x1 -> x2, waiting for transfers between devices: 261 us -> 651 us  [the longest x1 591 us: on_device(): lax.psum((grad_one, grad_two), ('sx', 'syz'))]
    unnamed x223 -> x89, local copies, waits for them, and re-layouts: 54.1 us -> 28.2 us
    ppermute x8, starting transfers between devices: 23.5 us -> 35 us  [from_behind(): lax.ppermute(value, axis, [(source, source + steps) for source in range(i...]
    dot_general x18, matrix products: 16.9 us -> 7.09 us  [data_grad(): jnp.einsum('xyzk,kc->xyzc', window, matrix, preferred_element_type=jnp.fl...]
  transfers between devices with their start and end apart: 9 -> 10, of which waited for: 4 -> 7; matrix products, arithmetic and copies ran while one was open for 21% -> 7% of each run, Pallas kernels for 0% -> 0%
where the time goes in v1:
time: 779 us; the launch traced here: 775 us
  waiting for transfers between devices  658 us (84%)
  local copies, waits for them, and re-layouts  38.1 us (5%)
  starting transfers between devices  35.1 us (5%)
  between operations  15.3 us (2%)
  matrix products  15.1 us (2%)
  other arithmetic  13.5 us (2%)
    psum x1, waiting for transfers between devices, on_device(): lax.psum((grad_one, grad_two), ('sx', 'syz'))  591 us
    psum x1, waiting for transfers between devices, on_device(): lax.psum(lax.psum((grad_one, grad_two), ('sx', 'syz')), 'dp')  60.2 us
    ppermute x8, starting transfers between devices, from_behind(): lax.ppermute(value, axis, [(source, source + steps) for source in range(i...  35 us
    unnamed x89, local copies, waits for them, and re-layouts  28.2 us
  transfers between devices with their start and end apart: 10, of which 7 were waited for; matrix products, arithmetic and copies ran while one was open for 7% of the time, Pallas kernels for 0%

profile of v1, /device:TPU:8, one launch (start us, length us, event | category | flops | bytes accessed | tf_op | source)
XLA Modules:
  0.0 775.4 jit_solution(1649851603468415719)
XLA Ops:
  7.2 3.4 collective-permute-start
  10.7 2.0 copy.221
  13.5 2.5 collective-permute-start.4
  17.7 1.3 collective-permute-start.1
  31.2 1.5 copy.282
  32.7 1.5 copy.281
  40.1 1.0 fusion.74
  42.0 0.9 fusion.67
  42.9 1.0 convolution_bitcast_fusion
  44.8 1.1 fusion.26
  45.9 1.0 fusion.30
  47.6 4.3 collective-permute-start.6
  51.9 1.1 fusion.25
  53.8 1.9 collective-permute-done.6
  56.4 4.5 collective-permute-start.7
  61.0 1.0 fusion.31
  62.7 1.2 fusion.23
  68.6 4.4 collective-permute-start.5
  73.0 1.4 broadcast_multiply_fusion
  74.4 1.2 collective-permute-done.5
  75.6 2.6 fusion.3
  78.3 1.4 fusion.342
  86.5 1.0 broadcast_multiply_fusion.1
  87.6 590.6 %all-reduce.27.cloned.1.call-done = (f32[3,3,3,64,128]{4,3,2,1,0:T(8,128)}, f32[3,3,3,128,128]{4,3,2,1,0:T(8,128)}) async-done(((f32[3,3,3,64,128]{4,3,2,1,0:T(8,128)}, f32[3,3,3,128,128]{4,3,2,1,0:T(8,128)}), (f32[3,3,3,64,128]{4,3,2,1,0:T(8,128)}, f32[3,3,3,128,128]{4,3,2,1,0:T(8,128)})) %all-reduce.27.cloned.1.call-update) | async-done | bytes 2654224 | tf_op jit(solution)/shard_map/psum | solution.py:109
  678.3 13.2 %collective-permute-start.2 = (bf16[1,8,64,128]{3,2,1,0:T(8,128)(2,1)S(1)}, bf16[1,8,64,128]{3,2,1,0:T(8,128)(2,1)S(1)}, u32[]{:S(2)}, u32[]{:S(2)}) collective-permute-start(bf16[1,8,64,128]{3,2,1,0:T(8,128)(2,1)S(1)} %slice.659), channel_id=1, source_target_pairs={{8,0},{16,8},{24,16},{32,24},{40,32},{48,40},{56,48},{9,1},{17,9},... | collective-permute-start | bytes 393224 | tf_op jit(solution)/shard_map/ppermute | solution.py:10
  691.6 2.5 collective-permute-done.2
  694.0 1.3 collective-permute-start.3
  698.7 1.3 collective-permute-done.3
  703.8 1.0 copy.220
  704.9 60.2 %all-reduce.29.cloned.1.call-done = (f32[3,3,3,64,128]{4,3,2,1,0:T(8,128)}, f32[3,3,3,128,128]{4,3,2,1,0:T(8,128)}) async-done(((f32[3,3,3,64,128]{4,3,2,1,0:T(8,128)}, f32[3,3,3,128,128]{4,3,2,1,0:T(8,128)}), (f32[3,3,3,64,128]{4,3,2,1,0:T(8,128)}, f32[3,3,3,128,128]{4,3,2,1,0:T(8,128)})) %all-reduce.29.cloned.1.call-update) | async-done | bytes 2654224 | tf_op jit(solution)/shard_map/psum | solution.py:109
  765.0 2.3 copy.390
  767.3 1.2 copy.391
  (200 shorter events, 43.3 us)
Async XLA Ops:
  7.2 671.1 %all-reduce.27.cloned.1.call-start = ((), (), s32[]{:S(2)}) async-start(), calls=%async_computation | async-start | bytes 5308416 | tf_op jit(solution)/shard_map/psum | solution.py:109
  7.2 8.9 %copy-start.1 = (bf16[1,2,8,64,128]{4,3,2,1,0:T(8,128)(2,1)S(1)}, bf16[1,2,8,64,128]{4,3,2,1,0:T(8,128)(2,1)}, u32[]{:S(2)}) copy-start(bf16[1,2,8,64,128]{4,3,2,1,0:T(8,128)(2,1)} %param.6) | copy-start | bytes 786436
  7.2 9.7 %copy-start.3 = (bf16[3,3,3,128,128]{4,3,2,1,0:T(8,128)(2,1)S(1)}, bf16[3,3,3,128,128]{4,3,2,1,0:T(8,128)(2,1)}, u32[]{:S(2)}) copy-start(bf16[3,3,3,128,128]{4,3,2,1,0:T(8,128)(2,1)} %param.9) | copy-start | bytes 2654212
  7.2 10.5 %collective-permute-start = (bf16[1,4,32,128]{3,2,1,0:T(8,128)(2,1)}, bf16[1,4,32,128]{3,2,1,0:T(8,128)(2,1)S(1)}, u32[]{:S(2)}, u32[]{:S(2)}) collective-permute-start(bf16[1,4,32,128]{3,2,1,0:T(8,128)(2,1)} %bitcast.710), channel_id=1, source_target_pairs={{8,0},{16,8},{24,16},{32,24},{40,32},{48,40},{56,48},{9,1},{17,9},... | collective-permute-start | bytes 98312 | tf_op jit(solution)/shard_map/ppermute | solution.py:10
  12.7 5.0 copy-start
  13.5 54.2 %collective-permute-start.4 = (bf16[1,16,64,128]{2,3,1,0:T(8,128)(2,1)}, bf16[1,16,64,128]{2,3,1,0:T(8,128)(2,1)}, u32[]{:S(2)}, u32[]{:S(2)}) collective-permute-start(bf16[1,16,64,128]{2,3,1,0:T(8,128)(2,1)} %slice_bitcast_fusion), channel_id=1, source_target_pairs={{0,8},{8,16},{16,24},{24,32},{32,40},{40,48},{48,56},{1,9},{9,17},... | collective-permute-start | bytes 786440 | tf_op jit(solution)/shard_map/ppermute | solution.py:10
  17.7 22.1 %collective-permute-start.1 = (bf16[2,1,32,128]{3,2,1,0:T(8,128)(2,1)S(1)}, bf16[2,1,32,128]{3,2,1,0:T(8,128)(2,1)S(1)}, u32[]{:S(2)}, u32[]{:S(2)}) collective-permute-start(bf16[2,1,32,128]{3,2,1,0:T(8,128)(2,1)S(1)} %pad_maximum_fusion.10), channel_id=1, source_target_pairs={{1,0},{2,1},{3,2},{4,3},{5,4},{6,5},{7,6},{9,8},{10,9},{11,10},{12... | collective-permute-start | bytes 49160 | tf_op jit(solution)/shard_map/ppermute | solution.py:10
  19.8 15.4 %copy-start.11 = (bf16[1,1,1,128,128]{4,3,2,1,0:T(8,128)(2,1)S(1)}, bf16[1,1,1,128,128]{4,3,2,1,0:T(8,128)(2,1)}, u32[]{:S(2)}) copy-start(bf16[1,1,1,128,128]{4,3,2,1,0:T(8,128)(2,1)} %get-tuple-element.40) | copy-start | bytes 98308
  19.8 15.6 %copy-start.10 = (bf16[1,1,1,128,128]{4,3,2,1,0:T(8,128)(2,1)S(1)}, bf16[1,1,1,128,128]{4,3,2,1,0:T(8,128)(2,1)}, u32[]{:S(2)}) copy-start(bf16[1,1,1,128,128]{4,3,2,1,0:T(8,128)(2,1)} %get-tuple-element.41) | copy-start | bytes 98308
  19.8 16.3 %copy-start.9 = (bf16[1,1,1,128,128]{4,3,2,1,0:T(8,128)(2,1)S(1)}, bf16[1,1,1,128,128]{4,3,2,1,0:T(8,128)(2,1)}, u32[]{:S(2)}) copy-start(bf16[1,1,1,128,128]{4,3,2,1,0:T(8,128)(2,1)} %get-tuple-element.42) | copy-start | bytes 98308
  19.8 17.1 %copy-start.8 = (bf16[1,1,1,128,128]{4,3,2,1,0:T(8,128)(2,1)S(1)}, bf16[1,1,1,128,128]{4,3,2,1,0:T(8,128)(2,1)}, u32[]{:S(2)}) copy-start(bf16[1,1,1,128,128]{4,3,2,1,0:T(8,128)(2,1)} %get-tuple-element.38) | copy-start | bytes 98308
  19.8 17.2 %copy-start.7 = (bf16[1,1,1,128,128]{4,3,2,1,0:T(8,128)(2,1)S(1)}, bf16[1,1,1,128,128]{4,3,2,1,0:T(8,128)(2,1)}, u32[]{:S(2)}) copy-start(bf16[1,1,1,128,128]{4,3,2,1,0:T(8,128)(2,1)} %get-tuple-element.39) | copy-start | bytes 98308
  19.8 17.9 %copy-start.6 = (bf16[1,1,1,128,128]{4,3,2,1,0:T(8,128)(2,1)S(1)}, bf16[1,1,1,128,128]{4,3,2,1,0:T(8,128)(2,1)}, u32[]{:S(2)}) copy-start(bf16[1,1,1,128,128]{4,3,2,1,0:T(8,128)(2,1)} %get-tuple-element.43) | copy-start | bytes 98308
  19.8 18.6 %copy-start.5 = (bf16[1,1,1,128,128]{4,3,2,1,0:T(8,128)(2,1)S(1)}, bf16[1,1,1,128,128]{4,3,2,1,0:T(8,128)(2,1)}, u32[]{:S(2)}) copy-start(bf16[1,1,1,128,128]{4,3,2,1,0:T(8,128)(2,1)} %get-tuple-element.37) | copy-start | bytes 98308
  41.2 0.8 copy-start.13
  41.6 2.3 copy-start.12
  47.6 8.1 %collective-permute-start.6 = (bf16[1,8,32,256]{3,2,1,0:T(8,128)(2,1)}, bf16[1,8,32,256]{3,2,1,0:T(8,128)(2,1)}, u32[]{:S(2)}, u32[]{:S(2)}) collective-permute-start(bf16[1,8,32,256]{3,2,1,0:T(8,128)(2,1)} %slice.626), channel_id=1, source_target_pairs={{0,8},{8,16},{16,24},{24,32},{32,40},{40,48},{48,56},{1,9},{9,17},... | collective-permute-start | bytes 393224 | tf_op jit(solution)/shard_map/ppermute | solution.py:10
  56.4 6.3 collective-permute-start.7
  68.6 7.1 collective-permute-start.5
  87.6 604.0 %copy-start.4 = (bf16[3,3,3,64,128]{4,3,2,1,0:T(8,128)(2,1)S(1)}, bf16[3,3,3,64,128]{4,3,2,1,0:T(8,128)(2,1)}, u32[]{:S(2)}) copy-start(bf16[3,3,3,64,128]{4,3,2,1,0:T(8,128)(2,1)} %param.8) | copy-start | bytes 1327108
  87.6 677.5 %all-reduce.29.cloned.1.call-start = ((), (), s32[]{:S(2)}) async-start(), calls=%async_computation.1 | async-start | bytes 5308416 | tf_op jit(solution)/shard_map/psum | solution.py:109
  678.3 15.8 %collective-permute-start.2 = (bf16[1,8,64,128]{3,2,1,0:T(8,128)(2,1)S(1)}, bf16[1,8,64,128]{3,2,1,0:T(8,128)(2,1)S(1)}, u32[]{:S(2)}, u32[]{:S(2)}) collective-permute-start(bf16[1,8,64,128]{3,2,1,0:T(8,128)(2,1)S(1)} %slice.659), channel_id=1, source_target_pairs={{8,0},{16,8},{24,16},{32,24},{40,32},{48,40},{56,48},{9,1},{17,9},... | collective-permute-start | bytes 393224 | tf_op jit(solution)/shard_map/ppermute | solution.py:10
  694.0 6.0 collective-permute-start.3
  765.0 2.3 copy-start.2
Sparse Core Ops, SparseCore 0:
  87.7 590.4 all-reduce.26
  681.0 84.0 all-reduce.28
